TPU v7x, 32 devices: a whole 2x2x4 slice. The times are simulated.
32 devices in a mesh: ens: 2 (over y), grid: 16 (over z, x, core).
Axes of the slice: x: 2, y: 2, z: 4, core: 2. Of those that a mesh axis runs over, the one named last changes fastest.
Arguments:
- fields: bfloat16 [2, 384, 768, 256], P('ens', 'grid'), may hold values from -6 to 6
- mode_counts: int32 [384], P('grid'), may hold values from 96 to 384, as said below
- gain_attn: float32 [256], replicated, may hold values from 0.5 to 1.5
- w_query: bfloat16 [256, 256], replicated, may hold values from -1 to 1
- w_key: bfloat16 [256, 256], replicated, may hold values from -8 to 8
- w_value: bfloat16 [256, 256], replicated, may hold values from -0.375 to 0.375
- w_out: bfloat16 [256, 256], replicated, may hold values from -0.375 to 0.375
- gain_spec: float32 [256], replicated, may hold values from 0.5 to 1.5
- w_first: bfloat16 [2, 8, 32, 32], replicated, may hold values from -1 to 1
- w_second: bfloat16 [2, 8, 32, 32], replicated, may hold values from -1 to 1
Outputs:
- layer_out: bfloat16 [2, 384, 768, 256], P('ens', 'grid')
Inputs may be any that keep to these rules, and one draw needn't show every extreme that they name: `mode_counts`: longitude wavenumbers kept in each latitude row; some row keeps all 384.
All inputs are finite; a program needn't handle non-finite values.
Results may differ from a plain program's by a relative error of at most 0.012.
Values may be sent and summed in bfloat16 or wider, within the bound.
A program may use at most 256 MiB of HBM per device.

v0:
```python
import math
import jax
import jax.numpy as jnp
from jax import lax
from jax.sharding import PartitionSpec as P

HEAD = 32
NLAT = 384
KLON = 384
KLAT = 128
norm_eps = 1e-05


def layer_norm(inputs, gain_vec):
    widened = inputs.astype(jnp.float32)
    center = widened - jnp.mean(widened, axis=-1, keepdims=True)
    spread = jnp.mean(center * center, axis=-1, keepdims=True)
    return center * lax.rsqrt(spread + norm_eps) * gain_vec


def lon_table(points, mode_count):
    positions = jnp.arange(points, dtype=jnp.int32)
    frequency = jnp.arange(mode_count, dtype=jnp.int32)
    turn_count = positions[:, None] * frequency[None, :] % points
    angles = 2.0 * math.pi / points * turn_count.astype(jnp.float32)
    factor = 1.0 / math.sqrt(points)
    return jnp.concatenate([jnp.cos(angles) * factor, -jnp.sin(angles) * factor], axis=1).astype(
        jnp.bfloat16
    )


def lon_inverse(points, mode_count):
    positions = jnp.arange(points, dtype=jnp.int32)
    frequency = jnp.arange(mode_count, dtype=jnp.int32)
    turn_count = frequency[:, None] * positions[None, :] % points
    angles = 2.0 * math.pi / points * turn_count.astype(jnp.float32)
    weight = jnp.where(frequency == 0, 1.0, 2.0).astype(jnp.float32)[:, None] / math.sqrt(points)
    return jnp.stack([jnp.cos(angles) * weight, -jnp.sin(angles) * weight]).astype(jnp.bfloat16)


def lat_angles(row_count, mode_count):
    frequency = jnp.arange(mode_count, dtype=jnp.int32)
    frequency = jnp.where(frequency < mode_count // 2, frequency, frequency - mode_count)
    positions = jnp.arange(row_count, dtype=jnp.int32)
    turn_count = frequency[:, None] * positions[None, :] % row_count
    return 2.0 * math.pi / row_count * turn_count.astype(jnp.float32)


def lat_forward(row_count, mode_count):
    angles = lat_angles(row_count, mode_count)
    factor = 1.0 / math.sqrt(row_count)
    cosine = jnp.cos(angles) * factor
    sine_part = jnp.sin(angles) * factor
    return jnp.stack(
        [jnp.stack([cosine, sine_part], axis=1), jnp.stack([-sine_part, cosine], axis=1)]
    ).astype(jnp.bfloat16)


def lat_inverse(row_count, mode_count):
    angles = jnp.transpose(lat_angles(row_count, mode_count))
    factor = 1.0 / math.sqrt(row_count)
    cosine = jnp.cos(angles) * factor
    sine_part = jnp.sin(angles) * factor
    return jnp.stack([jnp.stack([cosine, -sine_part]), jnp.stack([sine_part, cosine])]).astype(
        jnp.bfloat16
    )


def complex_blocks(weight):
    real_part = weight[0]
    imag_part = weight[1]
    return jnp.stack([jnp.stack([real_part, imag_part]), jnp.stack([-imag_part, real_part])])


def mix_blocks(spec, big):
    blocks = spec.reshape(spec.shape[:4] + (big.shape[2], big.shape[3]))
    out_blocks = jnp.einsum("mpqkbi,psbio->msqkbo", blocks, big, preferred_element_type=jnp.float32)
    return out_blocks.reshape(spec.shape)


def mix_members(all_scores, all_values, head_count):
    members, lat_rows, lon_points, feat_dim = all_values.shape
    row_max = jnp.max(all_scores, axis=0, keepdims=True)
    exps = jnp.exp(all_scores - row_max)
    totals = jnp.sum(exps, axis=0)
    weights = exps.astype(jnp.bfloat16)
    split_values = all_values.reshape(members, lat_rows, lon_points, head_count, HEAD)
    mixed_out = jnp.einsum(
        "nmlhw,nlwhe->mlwhe", weights, split_values, preferred_element_type=jnp.float32
    )
    mixed_out = mixed_out / jnp.transpose(totals, (0, 1, 3, 2))[..., None]
    return mixed_out.astype(jnp.bfloat16).reshape(
        all_scores.shape[1], lat_rows, lon_points, feat_dim
    )


def shards(
    fields, mode_counts, gain_attn, w_query, w_key, w_value, w_out, gain_spec, w_first, w_second
):
    mem_dev, lat_dev, lon_points, feat_dim = fields.shape
    head_count = feat_dim // HEAD
    score_scale = 1.0 / math.sqrt(HEAD)
    normed = layer_norm(fields, gain_attn).astype(jnp.bfloat16)
    queries = jnp.dot(normed, w_query, preferred_element_type=jnp.float32).astype(jnp.bfloat16)
    queries = queries.reshape(mem_dev, lat_dev, lon_points, head_count, HEAD)
    own_keys = jnp.dot(normed, w_key, preferred_element_type=jnp.float32).astype(jnp.bfloat16)
    own_values = jnp.dot(normed, w_value, preferred_element_type=jnp.float32).astype(jnp.bfloat16)
    key_rows = lax.all_gather(own_keys, "ens", axis=0, tiled=True)
    split_keys = key_rows.reshape(key_rows.shape[:3] + (head_count, HEAD))
    scores = (
        jnp.einsum("mlwhe,nlwhe->nmlhw", queries, split_keys, preferred_element_type=jnp.float32)
        * score_scale
    )
    all_values = lax.all_gather(own_values, "ens", axis=0, tiled=True)
    mixed_out = mix_members(scores, all_values, head_count)
    attended = (
        fields.astype(jnp.float32) + jnp.dot(mixed_out, w_out, preferred_element_type=jnp.float32)
    ).astype(jnp.bfloat16)
    retained = (jnp.arange(KLON, dtype=jnp.int32)[None, :] < mode_counts[:, None]).astype(
        jnp.float32
    )
    normed_two = layer_norm(attended, gain_spec).astype(jnp.bfloat16)
    spectrum = jnp.einsum(
        "mlxd,xk->mlkd", normed_two, lon_table(lon_points, KLON), preferred_element_type=jnp.float32
    )
    spectrum = spectrum.reshape(mem_dev, lat_dev, 2, KLON, feat_dim)
    spectrum = (spectrum * retained[None, :, None, :, None]).astype(jnp.bfloat16)
    forward = lat_forward(NLAT, KLAT)
    inverse = lat_inverse(NLAT, KLAT)
    big_one = complex_blocks(w_first)
    big_two = complex_blocks(w_second)
    rows_spec = jnp.einsum(
        "pqrj,mjrkd->mpqkd",
        forward,
        lax.all_to_all(spectrum, "grid", split_axis=3, concat_axis=1, tiled=True),
        preferred_element_type=jnp.float32,
    ).astype(jnp.bfloat16)
    hidden = jnp.maximum(mix_blocks(rows_spec, big_one), 0.0).astype(jnp.bfloat16)
    second = mix_blocks(hidden, big_two).astype(jnp.bfloat16)
    back_rows = jnp.einsum(
        "rpjq,mpqkd->mjrkd", inverse, second, preferred_element_type=jnp.float32
    ).astype(jnp.bfloat16)
    returned = lax.all_to_all(back_rows, "grid", split_axis=1, concat_axis=3, tiled=True)
    returned = returned * retained.astype(jnp.bfloat16)[None, :, None, :, None]
    field_out = jnp.einsum(
        "mjrkd,rkx->mjxd",
        returned,
        lon_inverse(lon_points, KLON),
        preferred_element_type=jnp.float32,
    )
    return (attended.astype(jnp.float32) + field_out).astype(jnp.bfloat16)


def solution(mesh):
    in_specs = (P("ens", "grid", None, None), P("grid"), P(), P(), P(), P(), P(), P(), P(), P())
    out_specs = P("ens", "grid", None, None)
    return jax.shard_map(shards, mesh=mesh, in_specs=in_specs, out_specs=out_specs, check_vma=False)
```

profile of v0, /device:TPU:11, one launch (start us, length us, event | category | flops | bytes accessed | tf_op | source)
XLA Modules:
  0.0 1163.1 jit_solution(6597510635387888419)
XLA Ops:
  6.5 12.6 %copy.142 = bf16[1,24,768,256]{2,3,1,0:T(8,128)(2,1)} copy(bf16[1,24,768,256]{3,2,1,0:T(8,128)(2,1)} %param.10) | data formatting | bytes 18874368 | tf_op args[0]
  19.2 5.2 convert_reduce_fusion.1
  24.4 1.2 copy-done.2
  25.5 2.6 fusion.7
  28.2 11.0 convolution_convert_fusion.1
  39.2 0.0 all-gather.7.cloned.1.call-update
  39.2 0.0 all-gather.5.cloned.1.call-start
  39.2 0.8 copy-done.11
  40.1 13.7 %convolution_convert_fusion.2 = bf16[24,768,256]{2,1,0:T(8,128)(2,1)} fusion(bf16[256,256]{1,0:T(8,128)(2,1)S(1)} %copy-done.11, bf16[1,24,768,256]{2,3,1,0:T(8,128)(2,1)} %copy.142, f32[256]{0:T(256)S(1)} %copy-done.8, f32[24,768]{1,0:T(8,128)S(1)} %add_rsqrt_fusion.1, f32[24,768]{1,0:T(8,128)S(1)} %broadcast_multiply_fusion.1), kind=kOutput, calls=%fused_computation.36 | convolution fusion | flops 2444230656 | bytes 19153920 | tf_op jit(solution)/shard_map/dot_general | solution.py:107
  53.8 0.0 all-gather.5.cloned.1.call-update
  53.8 5.3 multiply_convert_fusion.1
  59.1 0.7 fusion.85
  59.8 15.2 %bitcast_convert_fusion.3 = f32[24,8,768,32]{2,3,1,0:T(8,128)} fusion(bf16[256,256]{1,0:T(8,128)(2,1)S(1)} %copy-done.4, bf16[1,24,768,256]{2,3,1,0:T(8,128)(2,1)} %copy.142, f32[256]{0:T(256)S(1)} %copy-done.8, f32[24,768]{1,0:T(8,128)S(1)} %add_rsqrt_fusion.1, f32[24,768]{1,0:T(8,128)S(1)} %broadcast_multiply_fusion.1), kind=kOutput, calls=%fused_computation.143 | convolution fusion | flops 2448949248 | bytes 28591104 | tf_op jit(solution)/shard_map/dot_general | solution.py:104
  75.0 189.7 %all-gather.7.cloned.1.call-done = bf16[48,768,256]{2,1,0:T(8,128)(2,1)} async-done(((bf16[24,768,256]{2,1,0:T(8,128)(2,1)}), bf16[48,768,256]{2,1,0:T(8,128)(2,1)}) %all-gather.7.cloned.1.call-update) | async-done | bytes 18874384 | tf_op jit(solution)/shard_map/all_gather | solution.py:108
  264.7 24.2 %copy.207 = bf16[48,768,256]{1,2,0:T(8,128)(2,1)} copy(bf16[48,768,256]{2,1,0:T(8,128)(2,1)} %all-gather.7.cloned.1.call-done) | data formatting | bytes 37748736
  288.9 17.8 %multiply_reduce_fusion.1 = f32[24,8,768,2]{2,1,0,3:T(8,128)S(1)} fusion(bf16[24,8,768,32,2]{2,3,1,0,4:T(8,128)(2,1)} %bitcast.170, f32[24,8,768,32]{2,3,1,0:T(8,128)} %bitcast_convert_fusion.3), kind=kLoop, calls=%fused_computation.1 | loop fusion | flops 28016640 | bytes 38928384
  306.7 0.1 bitcast_reduce_fusion
  306.8 0.2 fusion.56
  307.1 183.5 %all-gather.5.cloned.1.call-done = bf16[48,768,256]{2,1,0:T(8,128)(2,1)} async-done(((bf16[24,768,256]{2,1,0:T(8,128)(2,1)}), bf16[48,768,256]{2,1,0:T(8,128)(2,1)}) %all-gather.5.cloned.1.call-update) | async-done | bytes 18874384 | tf_op jit(solution)/shard_map/all_gather | solution.py:114
  490.6 24.6 %copy.206 = bf16[48,768,256]{1,2,0:T(8,128)(2,1)} copy(bf16[48,768,256]{2,1,0:T(8,128)(2,1)} %all-gather.5.cloned.1.call-done) | data formatting | bytes 37748736
  515.2 13.5 %multiply_reduce_fusion = f32[24,768,8,32]{1,3,2,0:T(8,128)S(1)} fusion(bf16[24,768,8,2,32]{1,4,2,0,3:T(8,128)(2,1)} %bitcast.171, f32[24,768,8,2]{1,2,3,0:T(8,128)S(1)} %get-tuple-element.6), kind=kLoop, calls=%fused_computation | loop fusion | flops 23592960 | bytes 38928384 | tf_op jit(solution)/shard_map/nmlhw,nlwhe->mlwhe/dot_general | solution.py:88
  528.8 4.8 divide_convert_fusion
  533.6 20.6 %convert_reduce_fusion = (f32[24,768]{1,0:T(8,128)S(1)}, bf16[1,24,768,256]{2,3,1,0:T(8,128)(2,1)}) fusion(bf16[24,768,256]{1,2,0:T(8,128)(2,1)} %bitcast.172, bf16[256,256]{1,0:T(8,128)(2,1)S(1)} %copy-done, bf16[1,24,768,256]{2,3,1,0:T(8,128)(2,1)} %copy.142), kind=kOutput, calls=%fused_computation.4 | convolution fusion | flops 2439493632 | bytes 28516352 | tf_op jit(solution)/shard_map/dot_general | solution.py:117
  554.2 6.4 fusion.4
  560.6 10.8 fusion.15
  571.4 7.6 multiply_convert_fusion
  579.0 39.1 %copy.160 = bf16[1,24,2,384,256]{4,2,1,0,3:T(2,128)(2,1)} copy(bf16[1,24,2,384,256]{4,3,2,1,0:T(8,128)(2,1)S(1)} %multiply_convert_fusion) | data formatting | bytes 18874368 | tf_op jit(solution)/shard_map/convert_element_type | solution.py:127
  618.1 6.6 all-to-all-start
  624.8 0.1 copy.156
  624.9 0.1 copy.153
  625.2 0.9 fusion.78
  626.1 0.9 negate_convert_fusion
  627.0 202.5 %all-to-all-done = bf16[1,24,2,384,256]{4,2,1,0,3:T(2,128)(2,1)} async-done(((bf16[1,24,2,384,256]{4,2,1,0,3:T(2,128)(2,1)}), bf16[1,24,2,384,256]{4,2,1,0,3:T(2,128)(2,1)}, u32[]{:S(2)}, u32[]{:S(2)}) %all-to-all-start) | async-done | bytes 9437216 | tf_op jit(solution)/shard_map/all_to_all | solution.py:135
  829.6 10.7 copy.161
  840.3 8.3 copy.162
  848.6 19.5 %bitcast_convert_fusion.2 = bf16[24,256,2,128]{3,1,2,0:T(8,128)(2,1)S(1)} fusion(bf16[384,2,24,256,1]{3,2,1,0,4:T(8,128)(2,1)} %bitcast.178, bf16[1,128,2,384]{3,1,2,0:T(8,128)(2,1)S(1)} %get-tuple-element.14, bf16[1,128,2,384]{3,1,2,0:T(8,128)(2,1)S(1)} %get-tuple-element.13), kind=kOutput, calls=%fused_computation.40 | convolution fusion | flops 2418278400 | bytes 12976128 | tf_op jit(solution)/shard_map/pqrj,mjrkd->mpqkd/dot_general | solution.py:132
  868.1 1.0 fusion.28
  869.1 1.0 fusion.29
  870.1 1.0 copy.166
  871.1 5.3 fusion.12
  876.4 24.0 %copy.168 = bf16[1,384,2,24,256]{4,2,3,0,1:T(2,128)(2,1)} copy(bf16[1,384,2,24,256]{1,4,2,3,0:T(8,128)(2,1)} %fusion.12) | data formatting | bytes 18874368 | tf_op jit(solution)/shard_map/convert_element_type | solution.py:142
  900.3 5.2 all-to-all-start.1
  905.5 5.1 multiply_convert_fusion.4
  910.6 199.5 %all-to-all-done.1 = bf16[1,384,2,24,256]{4,2,3,0,1:T(2,128)(2,1)} async-done(((bf16[1,384,2,24,256]{4,2,3,0,1:T(2,128)(2,1)}), bf16[1,384,2,24,256]{4,2,3,0,1:T(2,128)(2,1)}, u32[]{:S(2)}, u32[]{:S(2)}) %all-to-all-start.1) | async-done | bytes 9437216 | tf_op jit(solution)/shard_map/all_to_all | solution.py:143
  1110.2 8.9 copy.169
  1119.1 8.6 copy.170
  1127.7 15.6 %fusion.11 = bf16[1,24,768,256]{2,3,1,0:T(8,128)(2,1)} fusion(bf16[1,24,768,256]{2,3,1,0:T(8,128)(2,1)} %get-tuple-element.26, bf16[24,2,384,256]{3,2,1,0:T(8,128)(2,1)} %bitcast.177, bf16[24,384]{1,0:T(8,128)(2,1)S(1)} %copy-done.7, bf16[1,384,768]{1,2,0:T(8,128)(2,1)S(1)} %get-tuple-element.16, bf16[1,384,768]{1,2,0:T(8,128)(2,1)S(1)} %get-tuple-element.15), kind=kOutput, calls=%fused_computation.19 | convolution fusion | flops 7283146752 | bytes 29509632 | tf_op jit(solution)/shard_map/mjrkd,rkx->mjxd/dot_general | solution.py:145
  1143.3 12.6 %copy.172 = bf16[1,24,768,256]{3,2,1,0:T(8,128)(2,1)} copy(bf16[1,24,768,256]{2,3,1,0:T(8,128)(2,1)} %fusion.11) | data formatting | bytes 18874368 | tf_op jit(solution)/shard_map/convert_element_type | solution.py:151
  (37 shorter events, 0.3 us)
Async XLA Ops:
  6.5 527.0 %copy-start = (bf16[256,256]{1,0:T(8,128)(2,1)S(1)}, bf16[256,256]{1,0:T(8,128)(2,1)}, u32[]{:S(2)}) copy-start(bf16[256,256]{1,0:T(8,128)(2,1)} %param.16) | copy-start | bytes 393220
  6.5 258.1 %all-gather.7.cloned.1.call-start = ((), (), s32[]{:S(2)}) async-start(), calls=%async_computation.3 | async-start | bytes 28311552 | tf_op jit(solution)/shard_map/all_gather | solution.py:108
  19.2 6.4 copy-start.2
  19.2 9.0 copy-start.8
  19.2 9.0 copy-start.10
  39.2 0.9 copy-start.11
  39.2 451.4 %all-gather.5.cloned.1.call-start = ((), (), s32[]{:S(2)}) async-start(), calls=%async_computation.2 | async-start | bytes 28311552 | tf_op jit(solution)/shard_map/all_gather | solution.py:114
  53.8 5.3 copy-start.9
  53.8 6.0 copy-start.4
  554.2 6.5 copy-start.3
  554.2 6.5 copy-start.12
  618.1 6.6 copy-start.5
  618.1 6.8 copy-start.6
  618.1 211.5 %all-to-all-start = ((bf16[1,24,2,384,256]{4,2,1,0,3:T(2,128)(2,1)}), bf16[1,24,2,384,256]{4,2,1,0,3:T(2,128)(2,1)}, u32[]{:S(2)}, u32[]{:S(2)}) async-start(bf16[1,24,2,384,256]{4,2,1,0,3:T(2,128)(2,1)} %copy.160), calls=%async_computation | async-start | bytes 18874368 | tf_op jit(solution)/shard_map/all_to_all | solution.py:135
  900.3 209.9 %all-to-all-start.1 = ((bf16[1,384,2,24,256]{4,2,3,0,1:T(2,128)(2,1)}), bf16[1,384,2,24,256]{4,2,3,0,1:T(2,128)(2,1)}, u32[]{:S(2)}, u32[]{:S(2)}) async-start(bf16[1,384,2,24,256]{4,2,3,0,1:T(2,128)(2,1)} %copy.168), calls=%async_computation.1 | async-start | bytes 18874368 | tf_op jit(solution)/shard_map/all_to_all | solution.py:143
  1119.1 8.6 copy-start.7
  1127.7 28.1 %copy-start.1 = (bf16[256,256]{1,0:T(8,128)(2,1)S(1)}, bf16[256,256]{1,0:T(8,128)(2,1)}, u32[]{:S(2)}) copy-start(bf16[256,256]{1,0:T(8,128)(2,1)} %param.16) | copy-start | bytes 393220
Sparse Core Ops, SparseCore 0:
  39.3 225.2 all-gather.6
  266.2 224.3 all-gather.4
where the time goes:
time: 1170 us; the launch traced here: 1160 us
  waiting for transfers between devices  775 us (66%)
  local copies, waits for them, and re-layouts  177 us (15%)
  matrix products  114 us (10%)
  other arithmetic  71.3 us (6%)
  between operations  14.1 us (1%)
  starting transfers between devices  11.8 us (1%)
    all_to_all x1, waiting for transfers between devices, shards(): lax.all_to_all(spectrum, 'grid', split_axis=3, concat_axis=1, tiled=True)  203 us
    all_to_all x1, waiting for transfers between devices, shards(): lax.all_to_all(back_rows, 'grid', split_axis=1, concat_axis=3, tiled=True)  200 us
    all_gather x1, waiting for transfers between devices, shards(): key_rows = lax.all_gather(own_keys, 'ens', axis=0, tiled=True)  190 us
    all_gather x1, waiting for transfers between devices, shards(): all_values = lax.all_gather(own_values, 'ens', axis=0, tiled=True)  184 us
    unnamed x31, local copies, waits for them, and re-layouts  63.8 us
    convert_element_type x1, local copies, waits for them, and re-layouts, shards(): (spectrum * retained[None, :, None, :, None]).astype(jnp.bfloat16)  39.1 us
    convert_element_type x1, local copies, waits for them, and re-layouts, shards(): back_rows = jnp.einsum('rpjq,mpqkd->mjrkd', inverse, second, preferred_el...  24 us
  transfers between devices with their start and end apart: 4, of which 4 were waited for; matrix products, arithmetic and copies ran while one was open for 7% of the time, Pallas kernels for 0%

commit v1 on v0

--- a/solution.py
+++ b/solution.py
@@ -111,7 +111,9 @@
         jnp.einsum("mlwhe,nlwhe->nmlhw", queries, split_keys, preferred_element_type=jnp.float32)
         * score_scale
     )
-    all_values = lax.all_gather(own_values, "ens", axis=0, tiled=True)
+    all_values = jnp.concatenate(
+        lax.all_to_all(jnp.stack([own_values] * lax.axis_size("ens")), "ens", 0, 0), axis=0
+    )
     mixed_out = mix_members(scores, all_values, head_count)
     attended = (
         fields.astype(jnp.float32) + jnp.dot(mixed_out, w_out, preferred_element_type=jnp.float32)

time: 1170 us -> 1200 us (1.026)
  other arithmetic: 71.3 us -> 99.3 us
    all_to_all x0 -> x1, waiting for transfers between devices: none -> 366 us  [shards(): lax.all_to_all(jnp.stack([own_values] * lax.axis_size('ens')), 'ens', 0, 0)]
    all_gather x1, waiting for transfers between devices: 190 us -> 0.01 us  [shards(): key_rows = lax.all_gather(own_keys, 'ens', axis=0, tiled=True)]
    all_gather x1 -> x0, waiting for transfers between devices: 184 us -> none  [shards(): all_values = lax.all_gather(own_values, 'ens', axis=0, tiled=True)]
    another operation x4 -> x5, other arithmetic: 12.2 us -> 29.7 us  [the longest x1 17.8 us: shards(): jnp.stack([own_values] * lax.axis_size('ens'))]
    unnamed x31 -> x41, local copies, waits for them, and re-layouts: 63.8 us -> 64.2 us
  transfers between devices with their start and end apart: 4 -> 4, of which waited for: 4 -> 3; matrix products, arithmetic and copies ran while one was open for 7% -> 7% of each run, Pallas kernels for 0% -> 0%
where the time goes in v1:
time: 1200 us; the launch traced here: 1190 us
  waiting for transfers between devices  768 us (64%)
  local copies, waits for them, and re-layouts  177 us (15%)
  matrix products  111 us (9%)
  other arithmetic  99.3 us (8%)
  starting transfers between devices  22.5 us (2%)
  between operations  14.2 us (1%)
    all_to_all x1, waiting for transfers between devices, shards(): lax.all_to_all(jnp.stack([own_values] * lax.axis_size('ens')), 'ens', 0, 0)  366 us
    all_to_all x1, waiting for transfers between devices, shards(): lax.all_to_all(spectrum, 'grid', split_axis=3, concat_axis=1, tiled=True)  203 us
    all_to_all x1, waiting for transfers between devices, shards(): lax.all_to_all(back_rows, 'grid', split_axis=1, concat_axis=3, tiled=True)  200 us
    unnamed x41, local copies, waits for them, and re-layouts  64.2 us
    convert_element_type x1, local copies, waits for them, and re-layouts, shards(): (spectrum * retained[None, :, None, :, None]).astype(jnp.bfloat16)  39.1 us
  transfers between devices with their start and end apart: 4, of which 3 were waited for; matrix products, arithmetic and copies ran while one was open for 7% of the time, Pallas kernels for 0%

profile of v1, /device:TPU:11, one launch (start us, length us, event | category | flops | bytes accessed | tf_op | source)
XLA Modules:
  0.0 1192.5 jit_solution(2181211197678035927)
XLA Ops:
  6.5 12.6 %copy.142 = bf16[1,24,768,256]{2,3,1,0:T(8,128)(2,1)} copy(bf16[1,24,768,256]{3,2,1,0:T(8,128)(2,1)} %param.10) | data formatting | bytes 18874368 | tf_op args[0]
  19.2 5.2 convert_reduce_fusion.1
  24.4 1.2 copy-done.2
  25.5 2.6 fusion.7
  28.2 11.1 convolution_convert_fusion.1
  39.3 0.0 all-gather.3.cloned.1.call-update
  39.3 0.9 copy-done.11
  40.2 13.7 %convert_bitcast_fusion = bf16[1,1,24,768,256]{4,3,2,1,0:T(8,128)(2,1)} fusion(bf16[256,256]{1,0:T(8,128)(2,1)S(1)} %copy-done.11, bf16[1,24,768,256]{2,3,1,0:T(8,128)(2,1)} %copy.142, f32[256]{0:T(256)S(1)} %copy-done.8, f32[24,768]{1,0:T(8,128)S(1)} %add_rsqrt_fusion.1, f32[24,768]{1,0:T(8,128)S(1)} %broadcast_multiply_fusion.1), kind=kOutput, calls=%fused_computation.35 | convolution fusion | flops 2444230656 | bytes 19153920 | tf_op jit(solution)/shard_map/dot_general | solution.py:107
  53.8 17.8 %pad_maximum_fusion = bf16[2,1,24,768,256]{4,3,2,1,0:T(8,128)(2,1)} fusion(bf16[1,1,24,768,256]{4,3,2,1,0:T(8,128)(2,1)} %convert_bitcast_fusion), kind=kLoop, calls=%fused_computation.20 | loop fusion | flops 9437184 | bytes 28311552 | tf_op jit(solution)/shard_map/stack | solution.py:115
  71.7 10.9 all-to-all-start
  82.5 5.0 multiply_convert_fusion.1
  87.6 0.7 fusion.85
  88.3 13.2 %bitcast_convert_fusion.3 = f32[24,8,768,32]{2,3,1,0:T(8,128)} fusion(bf16[256,256]{1,0:T(8,128)(2,1)S(1)} %copy-done.4, bf16[1,24,768,256]{2,3,1,0:T(8,128)(2,1)} %copy.142, f32[256]{0:T(256)S(1)} %copy-done.8, f32[24,768]{1,0:T(8,128)S(1)} %add_rsqrt_fusion.1, f32[24,768]{1,0:T(8,128)S(1)} %broadcast_multiply_fusion.1), kind=kOutput, calls=%fused_computation.144 | convolution fusion | flops 2448949248 | bytes 28591104 | tf_op jit(solution)/shard_map/dot_general | solution.py:104
  101.4 365.5 %all-to-all-done = bf16[2,1,24,768,256]{4,3,2,1,0:T(8,128)(2,1)} async-done(((bf16[2,1,24,768,256]{4,3,2,1,0:T(8,128)(2,1)}), bf16[2,1,24,768,256]{4,3,2,1,0:T(8,128)(2,1)}, u32[]{:S(2)}, u32[]{:S(2)}) %all-to-all-start) | async-done | bytes 18874400 | tf_op jit(solution)/shard_map/all_to_all | solution.py:115
  466.9 24.4 %copy.206 = bf16[2,1,24,768,256]{3,4,2,0,1:T(8,128)(2,1)} copy(bf16[2,1,24,768,256]{4,3,2,1,0:T(8,128)(2,1)} %all-to-all-done) | data formatting | bytes 37748736
  491.4 24.7 %copy.207 = bf16[48,768,256]{1,2,0:T(8,128)(2,1)} copy(bf16[48,768,256]{2,1,0:T(8,128)(2,1)} %all-gather.3.cloned.1.call-done) | data formatting | bytes 37748736
  516.1 19.4 %multiply_reduce_fusion.1 = f32[24,8,768,2]{2,1,0,3:T(8,128)S(1)} fusion(bf16[24,8,768,32,2]{2,3,1,0,4:T(8,128)(2,1)} %bitcast.175, f32[24,8,768,32]{2,3,1,0:T(8,128)} %bitcast_convert_fusion.3), kind=kLoop, calls=%fused_computation.1 | loop fusion | flops 28016640 | bytes 38928384
  535.6 0.1 bitcast_reduce_fusion
  535.7 0.2 fusion.56
  536.0 15.3 %multiply_reduce_fusion = f32[24,768,8,32]{1,3,2,0:T(8,128)} fusion(bf16[24,768,8,2,32]{1,4,2,0,3:T(8,128)(2,1)S(1)} %bitcast.174, f32[24,768,8,2]{1,2,3,0:T(8,128)S(1)} %get-tuple-element.6), kind=kLoop, calls=%fused_computation | loop fusion | flops 23592960 | bytes 38928384 | tf_op jit(solution)/shard_map/nmlhw,nlwhe->mlwhe/dot_general | solution.py:88
  551.3 11.9 divide_convert_fusion
  563.2 20.6 %convert_reduce_fusion = (f32[24,768]{1,0:T(8,128)S(1)}, bf16[1,24,768,256]{2,3,1,0:T(8,128)(2,1)}) fusion(bf16[24,768,256]{1,2,0:T(8,128)(2,1)} %bitcast.176, bf16[256,256]{1,0:T(8,128)(2,1)S(1)} %copy-done, bf16[1,24,768,256]{2,3,1,0:T(8,128)(2,1)} %copy.142), kind=kOutput, calls=%fused_computation.4 | convolution fusion | flops 2439493632 | bytes 28516352 | tf_op jit(solution)/shard_map/dot_general | solution.py:119
  583.7 0.0 copy-start.12
  583.8 6.4 fusion.4
  590.2 10.8 fusion.15
  601.0 7.6 multiply_convert_fusion
  608.6 39.1 %copy.160 = bf16[1,24,2,384,256]{4,2,1,0,3:T(2,128)(2,1)} copy(bf16[1,24,2,384,256]{4,3,2,1,0:T(8,128)(2,1)S(1)} %multiply_convert_fusion) | data formatting | bytes 18874368 | tf_op jit(solution)/shard_map/convert_element_type | solution.py:129
  647.7 6.5 all-to-all-start.1
  654.3 0.1 copy.156
  654.4 0.1 copy.153
  654.7 0.9 fusion.78
  655.6 0.9 negate_convert_fusion
  656.5 202.5 %all-to-all-done.1 = bf16[1,24,2,384,256]{4,2,1,0,3:T(2,128)(2,1)} async-done(((bf16[1,24,2,384,256]{4,2,1,0,3:T(2,128)(2,1)}), bf16[1,24,2,384,256]{4,2,1,0,3:T(2,128)(2,1)}, u32[]{:S(2)}, u32[]{:S(2)}) %all-to-all-start.1) | async-done | bytes 9437216 | tf_op jit(solution)/shard_map/all_to_all | solution.py:137
  859.1 10.8 copy.161
  869.8 8.3 copy.162
  878.1 19.5 %bitcast_convert_fusion.2 = bf16[24,256,2,128]{3,1,2,0:T(8,128)(2,1)S(1)} fusion(bf16[384,2,24,256,1]{3,2,1,0,4:T(8,128)(2,1)} %bitcast.182, bf16[1,128,2,384]{3,1,2,0:T(8,128)(2,1)S(1)} %get-tuple-element.14, bf16[1,128,2,384]{3,1,2,0:T(8,128)(2,1)S(1)} %get-tuple-element.13), kind=kOutput, calls=%fused_computation.41 | convolution fusion | flops 2418278400 | bytes 12976128 | tf_op jit(solution)/shard_map/pqrj,mjrkd->mpqkd/dot_general | solution.py:134
  897.6 1.0 fusion.28
  898.6 1.0 fusion.29
  899.6 1.0 copy.166
  900.6 5.1 fusion.12
  905.7 24.0 %copy.168 = bf16[1,384,2,24,256]{4,2,3,0,1:T(2,128)(2,1)} copy(bf16[1,384,2,24,256]{1,4,2,3,0:T(8,128)(2,1)} %fusion.12) | data formatting | bytes 18874368 | tf_op jit(solution)/shard_map/convert_element_type | solution.py:144
  929.7 5.2 all-to-all-start.2
  934.9 5.1 multiply_convert_fusion.4
  940.0 199.5 %all-to-all-done.2 = bf16[1,384,2,24,256]{4,2,3,0,1:T(2,128)(2,1)} async-done(((bf16[1,384,2,24,256]{4,2,3,0,1:T(2,128)(2,1)}), bf16[1,384,2,24,256]{4,2,3,0,1:T(2,128)(2,1)}, u32[]{:S(2)}, u32[]{:S(2)}) %all-to-all-start.2) | async-done | bytes 9437216 | tf_op jit(solution)/shard_map/all_to_all | solution.py:145
  1139.5 9.0 copy.169
  1148.5 8.6 copy.170
  1157.1 15.6 %fusion.11 = bf16[1,24,768,256]{2,3,1,0:T(8,128)(2,1)} fusion(bf16[1,24,768,256]{2,3,1,0:T(8,128)(2,1)} %get-tuple-element.26, bf16[24,2,384,256]{3,2,1,0:T(8,128)(2,1)} %bitcast.181, bf16[24,384]{1,0:T(8,128)(2,1)S(1)} %copy-done.7, bf16[1,384,768]{1,2,0:T(8,128)(2,1)S(1)} %get-tuple-element.16, bf16[1,384,768]{1,2,0:T(8,128)(2,1)S(1)} %get-tuple-element.15), kind=kOutput, calls=%fused_computation.19 | convolution fusion | flops 7283146752 | bytes 29509632 | tf_op jit(solution)/shard_map/mjrkd,rkx->mjxd/dot_general | solution.py:147
  1172.7 12.6 %copy.172 = bf16[1,24,768,256]{3,2,1,0:T(8,128)(2,1)} copy(bf16[1,24,768,256]{2,3,1,0:T(8,128)(2,1)} %fusion.11) | data formatting | bytes 18874368 | tf_op jit(solution)/shard_map/convert_element_type | solution.py:153
  (48 shorter events, 0.3 us)
Async XLA Ops:
  6.5 556.6 %copy-start = (bf16[256,256]{1,0:T(8,128)(2,1)S(1)}, bf16[256,256]{1,0:T(8,128)(2,1)}, u32[]{:S(2)}) copy-start(bf16[256,256]{1,0:T(8,128)(2,1)} %param.16) | copy-start | bytes 393220
  6.5 484.9 %all-gather.3.cloned.1.call-start = ((), (), s32[]{:S(2)}) async-start(), calls=%async_computation.3 | async-start | bytes 28311552 | tf_op jit(solution)/shard_map/all_gather | solution.py:108
  19.2 6.4 copy-start.2
  19.2 9.0 copy-start.8
  19.2 9.0 copy-start.10
  39.2 0.9 copy-start.11
  71.7 15.9 %copy-start.9 = (s32[24]{0:T(128)S(1)}, s32[24]{0:T(128)}, u32[]{:S(2)}) copy-start(s32[24]{0:T(128)} %param.11) | copy-start | bytes 292
  71.7 16.6 %copy-start.4 = (bf16[256,256]{1,0:T(8,128)(2,1)S(1)}, bf16[256,256]{1,0:T(8,128)(2,1)}, u32[]{:S(2)}) copy-start(bf16[256,256]{1,0:T(8,128)(2,1)} %param.13) | copy-start | bytes 393220
  71.7 395.3 %all-to-all-start = ((bf16[2,1,24,768,256]{4,3,2,1,0:T(8,128)(2,1)}), bf16[2,1,24,768,256]{4,3,2,1,0:T(8,128)(2,1)}, u32[]{:S(2)}, u32[]{:S(2)}) async-start(bf16[2,1,24,768,256]{4,3,2,1,0:T(8,128)(2,1)} %pad_maximum_fusion), calls=%async_computation | async-start | bytes 37748736 | tf_op jit(solution)/shard_map/all_to_all | solution.py:115
  516.1 19.8 %slice-start = ((s8[18874368]{0:T(1024)(128)(4,1)}), s8[4194304]{0:T(1024)(128)(4,1)S(1)}, s32[]{:S(2)}) async-start(s8[18874368]{0:T(1024)(128)(4,1)} %bitcast.172), calls=%async_computation.4 | async-start | bytes 8388608
  516.1 19.8 %slice-start.1 = ((s8[18874368]{0:T(1024)(128)(4,1)}), s8[4194304]{0:T(1024)(128)(4,1)S(1)}, s32[]{:S(2)}) async-start(s8[18874368]{0:T(1024)(128)(4,1)} %bitcast.172), calls=%async_computation.5 | async-start | bytes 8388608
  516.1 19.8 %slice-start.2 = ((s8[18874368]{0:T(1024)(128)(4,1)}), s8[4194304]{0:T(1024)(128)(4,1)S(1)}, s32[]{:S(2)}) async-start(s8[18874368]{0:T(1024)(128)(4,1)} %bitcast.172), calls=%async_computation.6 | async-start | bytes 8388608
  516.1 19.8 %slice-start.3 = ((s8[18874368]{0:T(1024)(128)(4,1)}), s8[4194304]{0:T(1024)(128)(4,1)S(1)}, s32[]{:S(2)}) async-start(s8[18874368]{0:T(1024)(128)(4,1)} %bitcast.172), calls=%async_computation.7 | async-start | bytes 8388608
  516.1 19.8 %slice-start.4 = ((s8[18874368]{0:T(1024)(128)(4,1)}), s8[2097152]{0:T(1024)(128)(4,1)S(1)}, s32[]{:S(2)}) async-start(s8[18874368]{0:T(1024)(128)(4,1)} %bitcast.172), calls=%async_computation.8 | async-start | bytes 4194304
  583.7 6.5 copy-start.3
  583.7 6.5 copy-start.12
  647.7 6.5 copy-start.5
  647.7 6.7 copy-start.6
  647.7 211.3 %all-to-all-start.1 = ((bf16[1,24,2,384,256]{4,2,1,0,3:T(2,128)(2,1)}), bf16[1,24,2,384,256]{4,2,1,0,3:T(2,128)(2,1)}, u32[]{:S(2)}, u32[]{:S(2)}) async-start(bf16[1,24,2,384,256]{4,2,1,0,3:T(2,128)(2,1)} %copy.160), calls=%async_computation.1 | async-start | bytes 18874368 | tf_op jit(solution)/shard_map/all_to_all | solution.py:137
  929.7 209.9 %all-to-all-start.2 = ((bf16[1,384,2,24,256]{4,2,3,0,1:T(2,128)(2,1)}), bf16[1,384,2,24,256]{4,2,3,0,1:T(2,128)(2,1)}, u32[]{:S(2)}, u32[]{:S(2)}) async-start(bf16[1,384,2,24,256]{4,2,3,0,1:T(2,128)(2,1)} %copy.168), calls=%async_computation.2 | async-start | bytes 18874368 | tf_op jit(solution)/shard_map/all_to_all | solution.py:145
  1148.5 8.6 copy-start.7
  1157.1 28.2 %copy-start.1 = (bf16[256,256]{1,0:T(8,128)(2,1)S(1)}, bf16[256,256]{1,0:T(8,128)(2,1)}, u32[]{:S(2)}) copy-start(bf16[256,256]{1,0:T(8,128)(2,1)} %param.16) | copy-start | bytes 393220
Sparse Core Ops, SparseCore 0:
  39.4 403.9 all-gather.2
